TPU v7x, 32 devices: a whole 2x2x4 slice. The times are simulated.
32 devices in a mesh: seq: 4 (over z), shard: 8 (over y, x, core).
Axes of the slice: x: 2, y: 2, z: 4, core: 2. Of those that a mesh axis runs over, the one named last changes fastest.
Arguments:
- frames: bfloat16 [8, 1024, 1536], P('shard', 'seq'), may hold values from -6 to 6
- text_states: bfloat16 [8, 64, 1536], P('shard'), may hold values from -6 to 6
- norm_gain: bfloat16 [3, 1536], P(None, 'shard'), may hold values from 0.5 to 1.5
- norm_bias: bfloat16 [3, 1536], P(None, 'shard'), may hold values from -3 to 3
- self_project: bfloat16 [3, 1536, 1536], P(None, 'shard'), may hold values from -0.15625 to 0.15625
- self_output: bfloat16 [1536, 1536], P('shard'), may hold values from -1.75 to 1.75
- cross_project: bfloat16 [3, 1536, 1536], P(None, 'shard'), may hold values from -0.15625 to 0.15625
- cross_output: bfloat16 [1536, 1536], P('shard'), may hold values from -0.625 to 0.625
- up_weight: bfloat16 [1536, 6144], P('shard'), may hold values from -0.15625 to 0.15625
- down_weight: bfloat16 [6144, 1536], P('shard'), may hold values from -0.078125 to 0.078125
- cotangent: bfloat16 [8, 1024, 1536], P('shard', 'seq'), may hold values from -6 to 6
Outputs:
- output: bfloat16 [8, 1024, 1536], P('shard', 'seq')
- frames_grad: float32 [8, 1024, 1536], P('shard', 'seq')
- text_grad: float32 [8, 64, 1536], P('shard')
- gain_grad: float32 [3, 1536], P(None, 'shard')
- bias_grad: float32 [3, 1536], P(None, 'shard')
- self_project_grad: float32 [3, 1536, 1536], P(None, 'shard')
- self_output_grad: float32 [1536, 1536], P('shard')
- cross_project_grad: float32 [3, 1536, 1536], P(None, 'shard')
- cross_output_grad: float32 [1536, 1536], P('shard')
- up_grad: float32 [1536, 6144], P('shard')
- down_grad: float32 [6144, 1536], P('shard')
All inputs are finite; a program needn't handle non-finite values.
Results may differ from a plain program's by a relative error of at most 0.022.
Values may be sent and summed in bfloat16 or wider, within the bound.
No kernel may reach another device: no remote copies, remote signals or barrier semaphores. Data moves between devices by JAX's collectives and lax.ppermute only.
A program may use at most 384 MiB of HBM per device.

v0:
```python
import jax
import jax.numpy as jnp
from jax import lax
from jax.sharding import PartitionSpec as P

HEAD_DIM = 64
QBLOCK = 512
EPSILON = 1e-05
MASKED_SCORE = -1e30


def layer_norm(hidden, gain, shift):
    center = hidden - jnp.mean(hidden, axis=-1, keepdims=True)
    spread = lax.rsqrt(jnp.mean(center * center, axis=-1, keepdims=True) + EPSILON)
    return center * spread * gain + shift


def exact_gelu(values):
    return jax.nn.gelu(values, approximate=False)


def contract(form, left, right):
    return jnp.einsum(form, left, right, preferred_element_type=jnp.float32)


def split_heads(values):
    return values.reshape(values.shape[:-1] + (values.shape[-1] // HEAD_DIM, HEAD_DIM))


def join_heads(values):
    return values.reshape(values.shape[:-2] + (values.shape[-2] * values.shape[-1],))


def causal_visible(start_row, row_count, stop_row):
    row_place = start_row + lax.broadcasted_iota(jnp.int32, (row_count, stop_row), 0)
    column_place = lax.broadcasted_iota(jnp.int32, (row_count, stop_row), 1)
    return column_place <= row_place


def block_scores(queries, key_rows, start_row, stop_row, scaling):
    scores = (
        contract("cqhe,ckhe->chqk", queries[:, start_row:stop_row], key_rows[:, :stop_row])
        * scaling
    )
    return jnp.where(
        causal_visible(start_row, stop_row - start_row, stop_row), scores, MASKED_SCORE
    )


def self_forward(queries, key_rows, value_rows, scaling):
    length = queries.shape[1]
    outputs = []
    totals = []
    for start_row in range(0, length, QBLOCK):
        stop_row = start_row + QBLOCK
        scores = block_scores(queries, key_rows, start_row, stop_row, scaling)
        largest = jnp.max(scores, axis=-1, keepdims=True)
        weights = jnp.exp(scores - largest)
        summed = jnp.sum(weights, axis=-1, keepdims=True)
        shares = (weights / summed).astype(jnp.bfloat16)
        outputs.append(contract("chqk,ckhe->cqhe", shares, value_rows[:, :stop_row]))
        totals.append(largest + jnp.log(summed))
    return (jnp.concatenate(outputs, axis=1), totals)


def self_backward(queries, key_rows, value_rows, totals, grad_out, scaling):
    length = queries.shape[1]
    grad_queries = []
    grad_keys = jnp.zeros(key_rows.shape, jnp.float32)
    grad_values = jnp.zeros(value_rows.shape, jnp.float32)
    for number, start_row in enumerate(range(0, length, QBLOCK)):
        stop_row = start_row + QBLOCK
        query_block = queries[:, start_row:stop_row]
        grad_block = grad_out[:, start_row:stop_row]
        scores = block_scores(queries, key_rows, start_row, stop_row, scaling)
        shares = jnp.exp(scores - totals[number])
        grad_shares = contract("cqhe,ckhe->chqk", grad_block, value_rows[:, :stop_row])
        centred = jnp.sum(shares * grad_shares, axis=-1, keepdims=True)
        grad_scores = (shares * (grad_shares - centred)).astype(jnp.bfloat16)
        grad_queries.append(
            contract("chqk,ckhe->cqhe", grad_scores, key_rows[:, :stop_row]) * scaling
        )
        grad_keys = grad_keys.at[:, :stop_row].add(
            contract("chqk,cqhe->ckhe", grad_scores, query_block) * scaling
        )
        grad_values = grad_values.at[:, :stop_row].add(
            contract("chqk,cqhe->ckhe", shares.astype(jnp.bfloat16), grad_block)
        )
    return (jnp.concatenate(grad_queries, axis=1), grad_keys, grad_values)


def cross_softmax(queries, key_rows, scaling):
    scores = contract("cfhe,cxhe->chxf", queries, key_rows) * scaling
    largest = jnp.max(scores, axis=2, keepdims=True)
    weights = jnp.exp(scores - largest)
    return weights / jnp.sum(weights, axis=2, keepdims=True)


def fetch_self(self_project, self_output, norm_gain, norm_bias):
    return (
        lax.all_gather(self_project, "shard", axis=1, tiled=True),
        lax.all_gather(self_output, "shard", axis=0, tiled=True),
        lax.all_gather(norm_gain, "shard", axis=1, tiled=True),
        lax.all_gather(norm_bias, "shard", axis=1, tiled=True),
    )


def fetch_cross(cross_project, cross_output):
    return (
        lax.all_gather(cross_project, "shard", axis=1, tiled=True),
        lax.all_gather(cross_output, "shard", axis=0, tiled=True),
    )


def fetch_mlp(up_weight, down_weight):
    return (
        lax.all_gather(up_weight, "shard", axis=0, tiled=True),
        lax.all_gather(down_weight, "shard", axis=0, tiled=True),
    )


def body(
    frames,
    text_states,
    norm_gain,
    norm_bias,
    self_project,
    self_output,
    cross_project,
    cross_output,
    up_weight,
    down_weight,
    cotangent,
):
    scaling = HEAD_DIM ** (-0.5)
    project_all, output_all, gain_all, bias_all = fetch_self(
        self_project, self_output, norm_gain, norm_bias
    )
    gains = gain_all.astype(jnp.float32)
    biases = bias_all.astype(jnp.float32)
    hidden = frames.astype(jnp.float32)
    normed_one, norm_pull_one = jax.vjp(layer_norm, hidden, gains[0], biases[0])
    inputs_one = normed_one.astype(jnp.bfloat16)
    projected = contract("cfd,jde->jcfe", inputs_one, project_all).astype(jnp.bfloat16)
    by_heads = lax.all_to_all(projected, "seq", split_axis=3, concat_axis=2, tiled=True)
    queries = split_heads(by_heads[0])
    key_rows = split_heads(by_heads[1])
    value_rows = split_heads(by_heads[2])
    attended_heads, totals = self_forward(queries, key_rows, value_rows, scaling)
    attended = lax.all_to_all(
        join_heads(attended_heads).astype(jnp.bfloat16),
        "seq",
        split_axis=1,
        concat_axis=2,
        tiled=True,
    )
    hidden_one = hidden + contract("cfd,de->cfe", attended, output_all)
    cross_all, cross_out_all = fetch_cross(cross_project, cross_output)
    normed_two, norm_pull_two = jax.vjp(layer_norm, hidden_one, gains[1], biases[1])
    inputs_two = normed_two.astype(jnp.bfloat16)
    cross_queries = contract("cfd,de->cfe", inputs_two, cross_all[0]).astype(jnp.bfloat16)
    cross_pairs = contract("cxd,jde->jcxe", text_states, cross_all[1:]).astype(jnp.bfloat16)
    text_keys = split_heads(cross_pairs[0])
    text_values = split_heads(cross_pairs[1])
    cross_shares = cross_softmax(split_heads(cross_queries), text_keys, scaling)
    cross_low = cross_shares.astype(jnp.bfloat16)
    mixed_text = join_heads(contract("chxf,cxhe->cfhe", cross_low, text_values)).astype(
        jnp.bfloat16
    )
    hidden_two = hidden_one + contract("cfd,de->cfe", mixed_text, cross_out_all)
    up_all, down_all = fetch_mlp(up_weight, down_weight)
    normed_three, norm_pull_three = jax.vjp(layer_norm, hidden_two, gains[2], biases[2])
    inputs_three = normed_three.astype(jnp.bfloat16)
    before_act = contract("cfd,dk->cfk", inputs_three, up_all)
    activated, gelu_pull = jax.vjp(exact_gelu, before_act)
    activated_low = activated.astype(jnp.bfloat16)
    result = hidden_two + contract("cfk,kd->cfd", activated_low, down_all)
    output = result.astype(jnp.bfloat16)
    up_all, down_all = fetch_mlp(up_weight, down_weight)
    grad_result = cotangent.astype(jnp.float32)
    grad_down = contract("cfk,cfd->kd", activated_low, cotangent)
    grad_act = contract("cfd,kd->cfk", cotangent, down_all)
    grad_before = gelu_pull(grad_act)[0].astype(jnp.bfloat16)
    grad_up = contract("cfd,cfk->dk", inputs_three, grad_before)
    grad_inputs_three = contract("cfk,dk->cfd", grad_before, up_all)
    grad_two_part, gain_three, bias_three = norm_pull_three(grad_inputs_three)
    grad_hidden_two = grad_result + grad_two_part
    up_share, down_share = (
        lax.psum_scatter(
            grad_up.astype(jnp.bfloat16), "shard", scatter_dimension=0, tiled=True
        ).astype(jnp.float32),
        lax.psum_scatter(
            grad_down.astype(jnp.bfloat16), "shard", scatter_dimension=0, tiled=True
        ).astype(jnp.float32),
    )
    cross_all, cross_out_all = fetch_cross(cross_project, cross_output)
    grad_low_two = grad_hidden_two.astype(jnp.bfloat16)
    grad_cross_out = contract("cfd,cfe->de", mixed_text, grad_low_two)
    grad_mixed = split_heads(
        contract("cfe,de->cfd", grad_low_two, cross_out_all).astype(jnp.bfloat16)
    )
    grad_shares = contract("cfhe,cxhe->chxf", grad_mixed, text_values)
    centred = jnp.sum(cross_shares * grad_shares, axis=2, keepdims=True)
    grad_scores = (cross_shares * (grad_shares - centred)).astype(jnp.bfloat16)
    grad_cross_query = join_heads(
        contract("chxf,cxhe->cfhe", grad_scores, text_keys) * scaling
    ).astype(jnp.bfloat16)
    grad_text_keys = join_heads(
        contract("chxf,cfhe->cxhe", grad_scores, split_heads(cross_queries)) * scaling
    )
    grad_text_values = join_heads(contract("chxf,cfhe->cxhe", cross_low, grad_mixed))
    grad_pairs = lax.psum(jnp.stack([grad_text_keys, grad_text_values]).astype(jnp.bfloat16), "seq")
    grad_text = contract("jcxe,jde->cxd", grad_pairs, cross_all[1:])
    grad_cross_pairs = contract("cxd,jcxe->jde", text_states, grad_pairs)
    grad_cross_first = contract("cfd,cfe->de", inputs_two, grad_cross_query)
    grad_inputs_two = contract("cfe,de->cfd", grad_cross_query, cross_all[0])
    grad_one_part, gain_two, bias_two = norm_pull_two(grad_inputs_two)
    grad_hidden_one = grad_hidden_two + grad_one_part
    cross_stack = jnp.concatenate([grad_cross_first[None], grad_cross_pairs], axis=0)
    cross_share, cross_out_share = (
        lax.psum_scatter(
            cross_stack.astype(jnp.bfloat16), "shard", scatter_dimension=1, tiled=True
        ).astype(jnp.float32),
        lax.psum_scatter(
            grad_cross_out.astype(jnp.bfloat16), "shard", scatter_dimension=0, tiled=True
        ).astype(jnp.float32),
    )
    project_all, output_all, gain_all, bias_all = fetch_self(
        self_project, self_output, norm_gain, norm_bias
    )
    grad_low_one = grad_hidden_one.astype(jnp.bfloat16)
    grad_self_out = contract("cfd,cfe->de", attended, grad_low_one)
    grad_attended = contract("cfe,de->cfd", grad_low_one, output_all).astype(jnp.bfloat16)
    grad_heads = lax.all_to_all(grad_attended, "seq", split_axis=2, concat_axis=1, tiled=True)
    grad_queries, grad_keys, grad_values = self_backward(
        queries, key_rows, value_rows, totals, split_heads(grad_heads), scaling
    )
    grad_stacked = jnp.stack(
        [join_heads(grad_queries), join_heads(grad_keys), join_heads(grad_values)]
    ).astype(jnp.bfloat16)
    grad_projected = lax.all_to_all(grad_stacked, "seq", split_axis=2, concat_axis=3, tiled=True)
    grad_self_project = contract("cfd,jcfe->jde", inputs_one, grad_projected)
    grad_inputs_one = contract("jcfe,jde->cfd", grad_projected, project_all)
    grad_zero_part, gain_one, bias_one = norm_pull_one(grad_inputs_one)
    grad_frames = grad_hidden_one + grad_zero_part
    gain_stack = jnp.stack([gain_one, gain_two, gain_three])
    bias_stack = jnp.stack([bias_one, bias_two, bias_three])
    project_share, output_share, gain_share, bias_share = (
        lax.psum_scatter(
            grad_self_project.astype(jnp.bfloat16), "shard", scatter_dimension=1, tiled=True
        ).astype(jnp.float32),
        lax.psum_scatter(
            grad_self_out.astype(jnp.bfloat16), "shard", scatter_dimension=0, tiled=True
        ).astype(jnp.float32),
        lax.psum_scatter(
            gain_stack.astype(jnp.bfloat16), "shard", scatter_dimension=1, tiled=True
        ).astype(jnp.float32),
        lax.psum_scatter(
            bias_stack.astype(jnp.bfloat16), "shard", scatter_dimension=1, tiled=True
        ).astype(jnp.float32),
    )
    summed_parts = (
        lax.psum(project_share.astype(jnp.bfloat16), "seq").astype(jnp.float32),
        lax.psum(output_share.astype(jnp.bfloat16), "seq").astype(jnp.float32),
        lax.psum(cross_share[:1].astype(jnp.bfloat16), "seq").astype(jnp.float32),
        lax.psum(cross_out_share.astype(jnp.bfloat16), "seq").astype(jnp.float32),
        lax.psum(up_share.astype(jnp.bfloat16), "seq").astype(jnp.float32),
        lax.psum(down_share.astype(jnp.bfloat16), "seq").astype(jnp.float32),
        lax.psum(gain_share.astype(jnp.bfloat16), "seq").astype(jnp.float32),
        lax.psum(bias_share.astype(jnp.bfloat16), "seq").astype(jnp.float32),
    )
    cross_final = jnp.concatenate([summed_parts[2], cross_share[1:]], axis=0)
    return (
        output,
        grad_frames,
        grad_text,
        summed_parts[6],
        summed_parts[7],
        summed_parts[0],
        summed_parts[1],
        cross_final,
        summed_parts[3],
        summed_parts[4],
        summed_parts[5],
    )


def solution(mesh):
    return jax.shard_map(
        body,
        mesh=mesh,
        in_specs=(
            P("shard", "seq", None),
            P("shard", None, None),
            P(None, "shard"),
            P(None, "shard"),
            P(None, "shard", None),
            P("shard", None),
            P(None, "shard", None),
            P("shard", None),
            P("shard", None),
            P("shard", None),
            P("shard", "seq", None),
        ),
        out_specs=(
            P("shard", "seq", None),
            P("shard", "seq", None),
            P("shard", None, None),
            P(None, "shard"),
            P(None, "shard"),
            P(None, "shard", None),
            P("shard", None),
            P(None, "shard", None),
            P("shard", None),
            P("shard", None),
            P("shard", None),
        ),
        check_vma=False,
    )
```

profile of v0, /device:TPU:0, one launch (start us, length us, event | category | flops | bytes accessed | tf_op | source)
XLA Modules:
  0.0 1739.3 jit_solution(10451731953631284153)
XLA Ops:
  11.2 10.4 all-gather
  21.7 9.2 all-gather.1
  31.7 59.6 %all-gather.9.cloned.1.call-done = bf16[3,1536,1536]{2,1,0:T(8,128)(2,1)} async-done(((bf16[3,192,1536]{2,1,0:T(8,128)(2,1)}), bf16[3,1536,1536]{2,1,0:T(8,128)(2,1)}) %all-gather.9.cloned.1.call-update) | async-done | bytes 14155792 | tf_op jit(solution)/shard_map/all_gather | solution.py:101
  91.4 9.3 fusion.27
  111.2 69.5 %all-to-all-done = bf16[3,1,256,1536]{2,0,1,3:T(4,128)(2,1)} async-done(((bf16[3,1,256,1536]{2,0,1,3:T(4,128)(2,1)}), bf16[3,1,256,1536]{2,0,1,3:T(4,128)(2,1)}, u32[]{:S(2)}, u32[]{:S(2)}) %all-to-all-start) | async-done | bytes 2359328 | tf_op jit(solution)/shard_map/all_to_all | solution.py:145
  210.0 5.5 reduce.59
  220.0 6.0 fusion.41
  228.0 11.9 all-to-all-done.1
  261.1 92.5 %all-gather.17.cloned.1.call-done = bf16[1536,6144]{1,0:T(8,128)(2,1)} async-done(((bf16[192,6144]{1,0:T(8,128)(2,1)}), bf16[1536,6144]{1,0:T(8,128)(2,1)}) %all-gather.17.cloned.1.call-update) | async-done | bytes 18874384 | tf_op jit(solution)/shard_map/all_gather | solution.py:117
  353.6 23.7 %multiply_convert_fusion.2 = (bf16[256,6144]{1,0:T(8,128)(2,1)}, f32[256,6144]{1,0:T(8,128)}, f32[256,6144]{1,0:T(8,128)}) fusion(bf16[1536,6144]{1,0:T(8,128)(2,1)} %all-gather.17.cloned.1.call-done, f32[1,256,1536]{2,1,0:T(8,128)S(1)} %get-tuple-element.192, f32[1536]{0:T(1024)S(1)} %get-tuple-element.161, f32[1536]{0:T(1024)S(1)} %get-tuple-element.206, ...), kind=kOutput, calls=%fused_computation.31 | convolution fusion | flops 4936040448 | bytes 36190208 | tf_op jit(solution)/shard_map/cfd,dk->cfk/dot_general | solution.py:23
  377.3 76.7 %all-gather.19.cloned.1.call-done = bf16[6144,1536]{1,0:T(8,128)(2,1)} async-done(((bf16[768,1536]{1,0:T(8,128)(2,1)}), bf16[6144,1536]{1,0:T(8,128)(2,1)}) %all-gather.19.cloned.1.call-update) | async-done | bytes 18874384 | tf_op jit(solution)/shard_map/all_gather | solution.py:118
  453.9 14.8 add_convert_fusion
  468.7 10.7 fusion.57
  506.5 7.0 copy.211
  513.5 24.0 %all-reduce.7.cloned.1.call-done = bf16[2,64,1536]{2,1,0:T(8,128)(2,1)} async-done(((bf16[2,64,1536]{2,1,0:T(8,128)(2,1)}), bf16[2,64,1536]{2,1,0:T(8,128)(2,1)}) %all-reduce.7.cloned.1.call-update) | async-done | bytes 393232 | tf_op jit(solution)/shard_map/psum | solution.py:212
  541.6 6.1 pad_maximum_fusion
  547.7 30.8 %copy.225 = bf16[3,1536,1536]{2,0,1:T(4,128)(2,1)} copy(bf16[3,1536,1536]{1,2,0:T(8,128)(2,1)} %pad_maximum_fusion) | data formatting | bytes 28311552
  578.5 17.0 copy.233
  607.5 8.2 reduce.60
  620.5 18.2 %all-to-all-done.2 = bf16[4,2,49152]{2,1,0:T(2,128)(2,1)S(1)} async-done(((bf16[4,2,49152]{2,1,0:T(2,128)(2,1)}), bf16[4,2,49152]{2,1,0:T(2,128)(2,1)S(1)}, u32[]{:S(2)}, u32[]{:S(2)}) %all-to-all-start.2) | async-done | bytes 786464 | tf_op jit(solution)/shard_map/all_to_all | solution.py:234
  645.1 6.2 fusion.55
  654.2 6.9 multiply_reduce_fusion.1
  661.2 6.7 multiply_convert_fusion.1
  669.3 6.8 multiply_reduce_fusion
  676.1 6.2 multiply_convert_fusion
  703.0 6.8 pad_maximum_fusion.1
  709.7 72.8 %all_to_all.60 = bf16[3,1,1024,384]{3,0,1,2:T(4,128)(2,1)S(1)} all-to-all(bf16[3,1,1024,384]{3,0,1,2:T(4,128)(2,1)S(1)} %pad_maximum_fusion.1), channel_id=1, replica_groups=mesh['seq'=4,'shard'=8] {'seq'}, dimensions={2} | all-to-all | bytes 4718592 | tf_op jit(solution)/shard_map/all_to_all | solution.py:241
  790.3 7.5 convert_bitcast_fusion
  797.7 30.8 %copy.223 = bf16[3,1536,1536]{2,0,1:T(4,128)(2,1)} copy(bf16[3,1536,1536]{1,2,0:T(8,128)(2,1)} %convert_bitcast_fusion) | data formatting | bytes 28311552
  828.6 17.0 copy.232
  846.1 5.4 convolution_convert_fusion.3
  851.6 6.0 convolution_convert_fusion.5
  858.2 12.6 convolution_convert_fusion.1
  870.9 11.4 convolution_convert_fusion
  885.5 7.4 fusion.54
  906.5 40.3 %reduce-scatter.29.cloned.1.call-done = bf16[192,4608]{1,0:T(8,128)(2,1)} async-done(((bf16[1536,4608]{1,0:T(8,128)(2,1)}), bf16[192,4608]{1,0:T(8,128)(2,1)}) %reduce-scatter.29.cloned.1.call-update) | async-done | bytes 1769488
  951.9 5.6 copy.224
  957.5 46.9 %reduce-scatter.19.cloned.1.call-done = bf16[192,1536]{1,0:T(8,128)(2,1)} async-done(((bf16[1536,1536]{1,0:T(8,128)(2,1)}), bf16[192,1536]{1,0:T(8,128)(2,1)}) %reduce-scatter.19.cloned.1.call-update) | async-done | bytes 589840 | tf_op jit(solution)/shard_map/reduce_scatter | solution.py:224
  1004.5 57.8 %reduce-scatter.17.cloned.1.call-done = bf16[192,1536]{1,0:T(8,128)(2,1)} async-done(((bf16[1536,1536]{1,0:T(8,128)(2,1)}), bf16[192,1536]{1,0:T(8,128)(2,1)}) %reduce-scatter.17.cloned.1.call-update) | async-done | bytes 589840 | tf_op jit(solution)/shard_map/reduce_scatter | solution.py:252
  1062.3 129.9 %reduce-scatter.21.cloned.1.call-done = bf16[192,6144]{1,0:T(8,128)(2,1)} async-done(((bf16[1536,6144]{1,0:T(8,128)(2,1)}), bf16[192,6144]{1,0:T(8,128)(2,1)}) %reduce-scatter.21.cloned.1.call-update) | async-done | bytes 2359312 | tf_op jit(solution)/shard_map/reduce_scatter | solution.py:189
  1192.2 130.1 %reduce-scatter.23.cloned.1.call-done = bf16[768,1536]{1,0:T(8,128)(2,1)} async-done(((bf16[6144,1536]{1,0:T(8,128)(2,1)}), bf16[768,1536]{1,0:T(8,128)(2,1)}) %reduce-scatter.23.cloned.1.call-update) | async-done | bytes 2359312 | tf_op jit(solution)/shard_map/reduce_scatter | solution.py:192
  1323.7 10.7 fusion.31
  1334.4 7.6 fusion.44
  1343.7 15.4 reduce-scatter.25.cloned.1.call-done
  1360.0 35.9 %reduce-scatter.27.cloned.1.call-done = bf16[192,3]{1,0:T(8,128)(2,1)} async-done(((bf16[1536,3]{1,0:T(8,128)(2,1)}), bf16[192,3]{1,0:T(8,128)(2,1)}) %reduce-scatter.27.cloned.1.call-update) | async-done | bytes 1168
  1396.8 11.9 all-reduce.2
  1414.7 297.1 %all-reduce.9.cloned.1.call-done = (bf16[3,192,1536]{1,2,0:T(8,128)(2,1)}, bf16[192,1536]{1,0:T(8,128)(2,1)}, bf16[1,192,1536]{1,2,0:T(8,128)(2,1)}, bf16[192,15...) async-done(((bf16[3,192,1536]{1,2,0:T(8,128)(2,1)}, bf16[192,1536]{1,0:T(8,128)(2,1)}, bf16[1,192,1536]{1,2,0:T(8,128)(2,1)}, ...) | async-done | bytes 8257552 | tf_op jit(solution)/shard_map/psum | solution.py:263
  1721.3 5.7 copy.213
  (356 shorter events, 207.0 us)
Async XLA Ops:
  7.2 212.9 %copy-start = (bf16[1,64,1536]{2,1,0:T(8,128)(2,1)S(1)}, bf16[1,64,1536]{2,1,0:T(8,128)(2,1)}, u32[]{:S(2)}) copy-start(bf16[1,64,1536]{2,1,0:T(8,128)(2,1)} %param.24) | copy-start | bytes 589828
  7.2 84.2 %all-gather.9.cloned.1.call-start = ((), (), s32[]{:S(2)}) async-start(), calls=%async_computation.12 | async-start | bytes 15925248 | tf_op jit(solution)/shard_map/all_gather | solution.py:101
  7.9 212.1 %all-gather.13.cloned.1.call-start = ((), (), s32[]{:S(2)}) async-start(), calls=%async_computation.14 | async-start | bytes 15925248 | tf_op jit(solution)/shard_map/all_gather | solution.py:110
  8.7 13.0 copy-start.90
  8.7 22.4 %copy-start.5 = (bf16[1,256,1536]{2,1,0:T(8,128)(2,1)S(1)}, bf16[1,256,1536]{2,1,0:T(8,128)(2,1)}, u32[]{:S(2)}) copy-start(bf16[1,256,1536]{2,1,0:T(8,128)(2,1)} %param.23) | copy-start | bytes 2359300
  8.7 232.6 %all-gather.11.cloned.1.call-start = ((), (), s32[]{:S(2)}) async-start(), calls=%async_computation.13 | async-start | bytes 5308416 | tf_op jit(solution)/shard_map/all_gather | solution.py:102
  9.4 247.2 %all-gather.15.cloned.1.call-start = ((), (), s32[]{:S(2)}) async-start(), calls=%async_computation.15 | async-start | bytes 5308416 | tf_op jit(solution)/shard_map/all_gather | solution.py:111
  10.0 343.6 %all-gather.17.cloned.1.call-start = ((), (), s32[]{:S(2)}) async-start(), calls=%async_computation.16 | async-start | bytes 21233664 | tf_op jit(solution)/shard_map/all_gather | solution.py:117
  10.6 443.3 %all-gather.19.cloned.1.call-start = ((), (), s32[]{:S(2)}) async-start(), calls=%async_computation.17 | async-start | bytes 21233664 | tf_op jit(solution)/shard_map/all_gather | solution.py:118
  31.1 69.6 %copy-start.54 = (f32[1536]{0:T(1024)}, f32[1536]{0:T(1024)S(1)}, u32[]{:S(2)}) copy-start(f32[1536]{0:T(1024)S(1)} %get-tuple-element.204) | copy-start | bytes 18436
  31.1 69.6 %copy-start.65 = (f32[1536]{0:T(1024)}, f32[1536]{0:T(1024)S(1)}, u32[]{:S(2)}) copy-start(f32[1536]{0:T(1024)S(1)} %get-tuple-element.163) | copy-start | bytes 18436
  31.1 214.7 %copy-start.67 = (f32[1536]{0:T(1024)}, f32[1536]{0:T(1024)S(1)}, u32[]{:S(2)}) copy-start(f32[1536]{0:T(1024)S(1)} %get-tuple-element.205) | copy-start | bytes 18436
  31.1 214.7 %copy-start.83 = (f32[1536]{0:T(1024)}, f32[1536]{0:T(1024)S(1)}, u32[]{:S(2)}) copy-start(f32[1536]{0:T(1024)S(1)} %get-tuple-element.162) | copy-start | bytes 18436
  31.1 322.4 %copy-start.56 = (f32[1536]{0:T(1024)}, f32[1536]{0:T(1024)S(1)}, u32[]{:S(2)}) copy-start(f32[1536]{0:T(1024)S(1)} %get-tuple-element.161) | copy-start | bytes 18436
  31.4 69.4 %copy-start.70 = (f32[256]{0:T(256)}, f32[256]{0:T(256)S(1)}, u32[]{:S(2)}) copy-start(f32[256]{0:T(256)S(1)} %broadcast_multiply_fusion.2) | copy-start | bytes 3076
  31.7 69.0 %copy-start.76 = (f32[256]{0:T(256)}, f32[256]{0:T(256)S(1)}, u32[]{:S(2)}) copy-start(f32[256]{0:T(256)S(1)} %fusion.53) | copy-start | bytes 3076
  31.7 69.0 %copy-start.72 = (f32[256]{0:T(256)}, f32[256]{0:T(256)S(1)}, u32[]{:S(2)}) copy-start(f32[256]{0:T(256)S(1)} %fusion.100) | copy-start | bytes 3076
  104.3 76.4 %all-to-all-start = ((bf16[3,1,256,1536]{2,0,1,3:T(4,128)(2,1)}), bf16[3,1,256,1536]{2,0,1,3:T(4,128)(2,1)}, u32[]{:S(2)}, u32[]{:S(2)}) async-start(bf16[3,1,256,1536]{2,0,1,3:T(4,128)(2,1)} %copy.187), calls=%async_computation | async-start | bytes 6291456 | tf_op jit(solution)/shard_map/all_to_all | solution.py:145
  187.2 8.9 copy-start.25
  189.2 14.4 copy-start.35
  216.4 23.5 %all-to-all-start.1 = ((bf16[4,2,49152]{2,1,0:T(2,128)(2,1)}), bf16[4,2,49152]{2,1,0:T(2,128)(2,1)S(1)}, u32[]{:S(2)}, u32[]{:S(2)}) async-start(bf16[4,2,49152]{2,1,0:T(2,128)(2,1)} %reshape.954), calls=%async_computation.1 | async-start | bytes 1572864 | tf_op jit(solution)/shard_map/all_to_all | solution.py:150
  220.0 317.6 %all-reduce.7.cloned.1.call-start = ((), (), s32[]{:S(2)}) async-start(), calls=%async_computation.18 | async-start | bytes 786432 | tf_op jit(solution)/shard_map/psum | solution.py:212
  254.0 237.8 %copy-start.58 = (f32[24,256]{1,0:T(8,128)}, f32[24,256]{1,0:T(8,128)S(1)}, u32[]{:S(2)}) copy-start(f32[24,256]{1,0:T(8,128)S(1)} %get-tuple-element.189) | copy-start | bytes 73732
  260.8 218.7 %copy-start.9 = (f32[1,256,1536]{2,1,0:T(8,128)}, f32[1,256,1536]{2,1,0:T(8,128)S(1)}, u32[]{:S(2)}) copy-start(f32[1,256,1536]{2,1,0:T(8,128)S(1)} %get-tuple-element.192) | copy-start | bytes 4718596
  500.4 396.8 %reduce-scatter.31.cloned.1.call-start = ((), (), s32[]{:S(2)}) async-start(), calls=%async_computation.26 | async-start | bytes 15925248
  595.6 9.2 slice-start.3
  596.7 8.1 slice-start.4
  607.4 13.0 copy-start.60
  607.5 13.0 copy-start.62
  607.5 13.0 copy-start.53
  607.5 13.0 copy-start.64
  616.7 22.0 %all-to-all-start.2 = ((bf16[4,2,49152]{2,1,0:T(2,128)(2,1)}), bf16[4,2,49152]{2,1,0:T(2,128)(2,1)S(1)}, u32[]{:S(2)}, u32[]{:S(2)}) async-start(bf16[4,2,49152]{2,1,0:T(2,128)(2,1)} %reshape.956), calls=%async_computation.2 | async-start | bytes 1572864 | tf_op jit(solution)/shard_map/all_to_all | solution.py:234
  620.5 326.3 %reduce-scatter.29.cloned.1.call-start = ((), (), s32[]{:S(2)}) async-start(), calls=%async_computation.25 | async-start | bytes 15925248
  641.0 13.3 copy-start.21
  645.1 9.1 copy-start.42
  654.2 14.7 slice-start
  654.2 14.7 slice-start.1
  661.2 7.8 slice-start.2
  845.6 158.8 %reduce-scatter.19.cloned.1.call-start = ((), (), s32[]{:S(2)}) async-start(), calls=%async_computation.20 | async-start | bytes 5308416 | tf_op jit(solution)/shard_map/reduce_scatter | solution.py:224
  851.5 210.8 %reduce-scatter.17.cloned.1.call-start = ((), (), s32[]{:S(2)}) async-start(), calls=%async_computation.19 | async-start | bytes 5308416 | tf_op jit(solution)/shard_map/reduce_scatter | solution.py:252
  857.6 334.7 %reduce-scatter.21.cloned.1.call-start = ((), (), s32[]{:S(2)}) async-start(), calls=%async_computation.21 | async-start | bytes 21233664 | tf_op jit(solution)/shard_map/reduce_scatter | solution.py:189
  870.8 451.5 %reduce-scatter.23.cloned.1.call-start = ((), (), s32[]{:S(2)}) async-start(), calls=%async_computation.22 | async-start | bytes 21233664 | tf_op jit(solution)/shard_map/reduce_scatter | solution.py:192
  882.3 476.8 %reduce-scatter.25.cloned.1.call-start = ((), (), s32[]{:S(2)}) async-start(), calls=%async_computation.23 | async-start | bytes 442368
  895.9 500.1 %reduce-scatter.27.cloned.1.call-start = ((), (), s32[]{:S(2)}) async-start(), calls=%async_computation.24 | async-start | bytes 442368
  897.0 814.8 %all-reduce.9.cloned.1.call-start = ((), (), s32[]{:S(2)}) async-start(), calls=%async_computation.27 | async-start | bytes 18087936 | tf_op jit(solution)/shard_map/psum | solution.py:263
  901.0 50.9 %copy-start.17 = (bf16[192,3,1536]{2,1,0:T(4,128)(2,1)}, bf16[192,3,1536]{2,1,0:T(4,128)(2,1)S(1)}, u32[]{:S(2)}) copy-start(bf16[192,3,1536]{2,1,0:T(4,128)(2,1)S(1)} %reshape.947) | copy-start | bytes 5308420
  1323.7 10.7 copy-start.43
  1342.0 67.9 %copy-start.18 = (bf16[192,3,1536]{2,1,0:T(4,128)(2,1)S(1)}, bf16[192,3,1536]{2,1,0:T(4,128)(2,1)}, u32[]{:S(2)}) copy-start(bf16[192,3,1536]{2,1,0:T(4,128)(2,1)} %copy-done.17) | copy-start | bytes 5308420
  (67 other events, 242.5 us)
Sparse Core Ops, SparseCore 0:
  9.9 81.4 all-gather.8
  93.3 78.6 all-gather.12
  173.8 38.7 all-gather.10
  214.4 38.7 all-gather.14
  255.0 98.5 all-gather.16
  355.3 98.5 all-gather.18
  500.6 36.9 all-reduce.6
  595.7 101.5 reduce-scatter.30
  845.8 100.9 reduce-scatter.28
  950.6 53.7 reduce-scatter.18
  1008.5 53.7 reduce-scatter.16
  1065.8 126.4 reduce-scatter.20
  1195.8 126.4 reduce-scatter.22
  1325.2 33.8 reduce-scatter.24
  1362.0 33.8 reduce-scatter.26
  1399.6 312.1 all-reduce.8
where the time goes:
time: 1750 us; the launch traced here: 1740 us
  waiting for transfers between devices  1110 us (63%)
  matrix products  220 us (13%)
  local copies, waits for them, and re-layouts  207 us (12%)
  blocking collectives  104 us (6%)
  other arithmetic  70.1 us (4%)
    psum x1, waiting for transfers between devices, body(): lax.psum(project_share.astype(jnp.bfloat16), 'seq').astype(jnp.float32)  297 us
    dot_general x38, matrix products, contract(): return jnp.einsum(form, left, right, preferred_element_type=jnp.float32)  218 us
    unnamed x214, local copies, waits for them, and re-layouts  146 us
    reduce_scatter x1, waiting for transfers between devices, body(): lax.psum_scatter(grad_down.astype(jnp.bfloat16), 'shard', scatter_dimensi...  130 us
    reduce_scatter x1, waiting for transfers between devices, body(): lax.psum_scatter(grad_up.astype(jnp.bfloat16), 'shard', scatter_dimension...  130 us
    unnamed x20, waiting for transfers between devices  95.5 us
    all_gather x1, waiting for transfers between devices, fetch_mlp(): lax.all_gather(up_weight, 'shard', axis=0, tiled=True)  92.5 us
    all_gather x1, waiting for transfers between devices, fetch_mlp(): lax.all_gather(down_weight, 'shard', axis=0, tiled=True)  76.7 us
  transfers between devices with their start and end apart: 19, of which 15 were waited for; matrix products, arithmetic and copies ran while one was open for 21% of the time, Pallas kernels for 0%

commit v1 on v0

--- a/solution.py
+++ b/solution.py
@@ -259,8 +259,12 @@
             bias_stack.astype(jnp.bfloat16), "shard", scatter_dimension=1, tiled=True
         ).astype(jnp.float32),
     )
+
+    def _try_all_tails(target):
+        return lax.all_gather(target, "seq").sum(axis=0)
+
     summed_parts = (
-        lax.psum(project_share.astype(jnp.bfloat16), "seq").astype(jnp.float32),
+        _try_all_tails(project_share.astype(jnp.bfloat16)).astype(jnp.float32),
         lax.psum(output_share.astype(jnp.bfloat16), "seq").astype(jnp.float32),
         lax.psum(cross_share[:1].astype(jnp.bfloat16), "seq").astype(jnp.float32),
         lax.psum(cross_out_share.astype(jnp.bfloat16), "seq").astype(jnp.float32),

time: 1750 us -> 1650 us (0.943)
  waiting for transfers between devices: 1110 us -> 995 us
    all_gather x0 -> x1, waiting for transfers between devices: none -> 110 us  [_try_all_tails(): return lax.all_gather(target, 'seq').sum(axis=0)]
    reduce_scatter x1, waiting for transfers between devices: 130 us -> 29.4 us  [body(): lax.psum_scatter(grad_up.astype(jnp.bfloat16), 'shard', scatter_dimension...]
    psum x1, waiting for transfers between devices: 297 us -> 220 us  [body(): lax.psum(output_share.astype(jnp.bfloat16), 'seq').astype(jnp.float32)]
    reduce_scatter x1, waiting for transfers between devices: 57.8 us -> 0.01 us  [body(): lax.psum_scatter(grad_self_out.astype(jnp.bfloat16), 'shard', scatter_dim...]
    unnamed x20 -> x21, waiting for transfers between devices: 95.5 us -> 153 us
    reduce_scatter x1, waiting for transfers between devices: 46.9 us -> 0.01 us  [body(): lax.psum_scatter(grad_cross_out.astype(jnp.bfloat16), 'shard', scatter_di...]
    unnamed x214 -> x202, local copies, waits for them, and re-layouts: 146 us -> 144 us
  transfers between devices with their start and end apart: 19 -> 20, of which waited for: 15 -> 14; matrix products, arithmetic and copies ran while one was open for 21% -> 23% of each run, Pallas kernels for 0% -> 0%
where the time goes in v1:
time: 1650 us; the launch traced here: 1640 us
  waiting for transfers between devices  995 us (60%)
  matrix products  225 us (14%)
  local copies, waits for them, and re-layouts  207 us (13%)
  blocking collectives  105 us (6%)
  other arithmetic  78.6 us (5%)
    dot_general x38, matrix products, contract(): return jnp.einsum(form, left, right, preferred_element_type=jnp.float32)  223 us
    psum x1, waiting for transfers between devices, body(): lax.psum(output_share.astype(jnp.bfloat16), 'seq').astype(jnp.float32)  220 us
    unnamed x21, waiting for transfers between devices  153 us
    unnamed x202, local copies, waits for them, and re-layouts  144 us
    reduce_scatter x1, waiting for transfers between devices, body(): lax.psum_scatter(grad_down.astype(jnp.bfloat16), 'shard', scatter_dimensi...  130 us
    all_gather x1, waiting for transfers between devices, _try_all_tails(): return lax.all_gather(target, 'seq').sum(axis=0)  110 us
    all_gather x1, waiting for transfers between devices, fetch_mlp(): lax.all_gather(up_weight, 'shard', axis=0, tiled=True)  93.7 us
    all_gather x1, waiting for transfers between devices, fetch_mlp(): lax.all_gather(down_weight, 'shard', axis=0, tiled=True)  76.6 us
  transfers between devices with their start and end apart: 20, of which 14 were waited for; matrix products, arithmetic and copies ran while one was open for 23% of the time, Pallas kernels for 0%

profile of v1, /device:TPU:0, one launch (start us, length us, event | category | flops | bytes accessed | tf_op | source)
XLA Modules:
  0.0 1640.1 jit_solution(5969772384294088082)
XLA Ops:
  11.2 10.4 all-gather.1
  21.7 9.2 all-gather.2
  31.7 59.6 %all-gather.11.cloned.1.call-done = bf16[3,1536,1536]{2,1,0:T(8,128)(2,1)} async-done(((bf16[3,192,1536]{2,1,0:T(8,128)(2,1)}), bf16[3,1536,1536]{2,1,0:T(8,128)(2,1)}) %all-gather.11.cloned.1.call-update) | async-done | bytes 14155792 | tf_op jit(solution)/shard_map/all_gather | solution.py:101
  91.4 9.3 fusion.27
  104.3 5.2 all-to-all-start
  111.4 69.5 %all-to-all-done = bf16[3,1,256,1536]{2,0,1,3:T(4,128)(2,1)} async-done(((bf16[3,1,256,1536]{2,0,1,3:T(4,128)(2,1)}), bf16[3,1,256,1536]{2,0,1,3:T(4,128)(2,1)}, u32[]{:S(2)}, u32[]{:S(2)}) %all-to-all-start) | async-done | bytes 2359328 | tf_op jit(solution)/shard_map/all_to_all | solution.py:145
  210.0 5.4 reduce.60
  220.0 6.0 fusion.41
  228.0 11.8 all-to-all-done.1
  259.9 93.7 %all-gather.19.cloned.1.call-done = bf16[1536,6144]{1,0:T(8,128)(2,1)} async-done(((bf16[192,6144]{1,0:T(8,128)(2,1)}), bf16[1536,6144]{1,0:T(8,128)(2,1)}) %all-gather.19.cloned.1.call-update) | async-done | bytes 18874384 | tf_op jit(solution)/shard_map/all_gather | solution.py:117
  353.6 23.7 %multiply_convert_fusion.2 = (bf16[256,6144]{1,0:T(8,128)(2,1)}, f32[256,6144]{1,0:T(8,128)}, f32[256,6144]{1,0:T(8,128)}) fusion(bf16[1536,6144]{1,0:T(8,128)(2,1)} %all-gather.19.cloned.1.call-done, f32[1,256,1536]{2,1,0:T(8,128)S(1)} %get-tuple-element.191, f32[1536]{0:T(1024)S(1)} %get-tuple-element.161, f32[1536]{0:T(1024)S(1)} %get-tuple-element.205, ...), kind=kOutput, calls=%fused_computation.31 | convolution fusion | flops 4936040448 | bytes 36190208 | tf_op jit(solution)/shard_map/cfd,dk->cfk/dot_general | solution.py:23
  377.3 76.6 %all-gather.21.cloned.1.call-done = bf16[6144,1536]{1,0:T(8,128)(2,1)} async-done(((bf16[768,1536]{1,0:T(8,128)(2,1)}), bf16[6144,1536]{1,0:T(8,128)(2,1)}) %all-gather.21.cloned.1.call-update) | async-done | bytes 18874384 | tf_op jit(solution)/shard_map/all_gather | solution.py:118
  453.9 15.3 add_convert_fusion
  469.2 10.7 fusion.57
  505.6 5.2 fusion.8
  510.8 6.8 copy.216
  517.6 22.6 %all-reduce.7.cloned.1.call-done = bf16[2,64,1536]{2,1,0:T(8,128)(2,1)} async-done(((bf16[2,64,1536]{2,1,0:T(8,128)(2,1)}), bf16[2,64,1536]{2,1,0:T(8,128)(2,1)}) %all-reduce.7.cloned.1.call-update) | async-done | bytes 393232 | tf_op jit(solution)/shard_map/psum | solution.py:212
  544.2 6.1 pad_maximum_fusion
  550.3 31.0 %copy.230 = bf16[3,1536,1536]{2,0,1:T(4,128)(2,1)} copy(bf16[3,1536,1536]{1,2,0:T(8,128)(2,1)} %pad_maximum_fusion) | data formatting | bytes 28311552
  581.3 17.0 %copy.240 = bf16[192,8,3,1536]{3,1,2,0:T(8,128)(2,1)} copy(bf16[192,8,3,1536]{3,2,1,0:T(4,128)(2,1)} %bitcast.329) | data formatting | bytes 28311552
  617.2 11.8 convolution_convert_fusion.1
  629.1 12.5 convolution_convert_fusion
  648.3 8.1 reduce.61
  662.1 18.7 %all-to-all-done.2 = bf16[4,2,49152]{2,1,0:T(2,128)(2,1)S(1)} async-done(((bf16[4,2,49152]{2,1,0:T(2,128)(2,1)}), bf16[4,2,49152]{2,1,0:T(2,128)(2,1)S(1)}, u32[]{:S(2)}, u32[]{:S(2)}) %all-to-all-start.2) | async-done | bytes 786464 | tf_op jit(solution)/shard_map/all_to_all | solution.py:234
  687.5 6.2 fusion.55
  696.5 6.8 multiply_reduce_fusion.1
  703.3 6.5 multiply_convert_fusion.1
  711.3 6.8 multiply_reduce_fusion
  718.1 6.3 multiply_convert_fusion
  745.2 6.8 pad_maximum_fusion.1
  752.0 73.0 %all_to_all.60 = bf16[3,1,1024,384]{3,0,1,2:T(4,128)(2,1)S(1)} all-to-all(bf16[3,1,1024,384]{3,0,1,2:T(4,128)(2,1)S(1)} %pad_maximum_fusion.1), channel_id=1, replica_groups=mesh['seq'=4,'shard'=8] {'seq'}, dimensions={2} | all-to-all | bytes 4718592 | tf_op jit(solution)/shard_map/all_to_all | solution.py:241
  833.0 9.8 convert_bitcast_fusion
  842.8 31.5 %copy.228 = bf16[3,1536,1536]{2,0,1:T(4,128)(2,1)} copy(bf16[3,1536,1536]{1,2,0:T(8,128)(2,1)} %convert_bitcast_fusion) | data formatting | bytes 28311552
  874.2 17.4 %copy.239 = bf16[192,8,3,1536]{3,1,2,0:T(8,128)(2,1)} copy(bf16[192,8,3,1536]{3,2,1,0:T(4,128)(2,1)} %bitcast.330) | data formatting | bytes 28311552
  894.9 8.0 fusion.54
  916.2 29.4 %reduce-scatter.21.cloned.1.call-done = bf16[192,6144]{1,0:T(8,128)(2,1)} async-done(((bf16[1536,6144]{1,0:T(8,128)(2,1)}), bf16[192,6144]{1,0:T(8,128)(2,1)}) %reduce-scatter.21.cloned.1.call-update) | async-done | bytes 2359312 | tf_op jit(solution)/shard_map/reduce_scatter | solution.py:189
  945.7 129.9 %reduce-scatter.23.cloned.1.call-done = bf16[768,1536]{1,0:T(8,128)(2,1)} async-done(((bf16[6144,1536]{1,0:T(8,128)(2,1)}), bf16[768,1536]{1,0:T(8,128)(2,1)}) %reduce-scatter.23.cloned.1.call-update) | async-done | bytes 2359312 | tf_op jit(solution)/shard_map/reduce_scatter | solution.py:192
  1075.7 105.3 %reduce-scatter.29.cloned.1.call-done = bf16[192,4608]{1,0:T(8,128)(2,1)} async-done(((bf16[1536,4608]{1,0:T(8,128)(2,1)}), bf16[192,4608]{1,0:T(8,128)(2,1)}) %reduce-scatter.29.cloned.1.call-update) | async-done | bytes 1769488
  1181.0 5.2 reshape.946
  1189.6 10.9 fusion.31
  1200.5 7.6 fusion.44
  1209.8 8.0 reduce-scatter.25.cloned.1.call-done
  1218.7 35.9 %reduce-scatter.27.cloned.1.call-done = bf16[192,3]{1,0:T(8,128)(2,1)} async-done(((bf16[1536,3]{1,0:T(8,128)(2,1)}), bf16[192,3]{1,0:T(8,128)(2,1)}) %reduce-scatter.27.cloned.1.call-update) | async-done | bytes 1168
  1255.5 12.0 all-reduce.2
  1273.5 220.0 %all-reduce.9.cloned.1.call-done = (bf16[192,1536]{1,0:T(8,128)(2,1)}, bf16[1,192,1536]{1,2,0:T(8,128)(2,1)}, bf16[192,1536]{1,0:T(8,128)(2,1)}, bf16[192,6144]{1,0:T(8,128)(2,1)}, bf16[768,1536]{1,0:T(8,128)(2,1)}) async-done(((bf16[192,1536]{1,0:T(8,128)(2,1)}, bf16[1,192,1536]{1,2,0:T(8,128)(2,1)}, bf16[192,1536]{1,0:T(8,128)(2,1)}, bf16[192,6144]{1,0:T(8,128)(2,1)}, bf16[768,1536]{1,0:T(8,128)(2,1)}), ...) | async-done | bytes 6488080 | tf_op jit(solution)/shard_map/psum | solution.py:268
  1500.7 6.2 copy.218
  1512.5 109.6 %all-gather.23.cloned.1.call-done = bf16[12,192,1536]{2,1,0:T(8,128)(2,1)} async-done(((bf16[3,192,1536]{2,1,0:T(8,128)(2,1)}), bf16[12,192,1536]{2,1,0:T(8,128)(2,1)}) %all-gather.23.cloned.1.call-update) | async-done | bytes 7077904 | tf_op jit(solution)/shard_map/all_gather | solution.py:264
  1622.0 5.8 reduce_sum.300
  (348 shorter events, 213.5 us)
Async XLA Ops:
  7.2 212.8 %copy-start = (bf16[1,64,1536]{2,1,0:T(8,128)(2,1)S(1)}, bf16[1,64,1536]{2,1,0:T(8,128)(2,1)}, u32[]{:S(2)}) copy-start(bf16[1,64,1536]{2,1,0:T(8,128)(2,1)} %param.24) | copy-start | bytes 589828
  7.2 84.2 %all-gather.11.cloned.1.call-start = ((), (), s32[]{:S(2)}) async-start(), calls=%async_computation.12 | async-start | bytes 15925248 | tf_op jit(solution)/shard_map/all_gather | solution.py:101
  7.9 212.1 %all-gather.15.cloned.1.call-start = ((), (), s32[]{:S(2)}) async-start(), calls=%async_computation.14 | async-start | bytes 15925248 | tf_op jit(solution)/shard_map/all_gather | solution.py:110
  8.7 13.0 copy-start.86
  8.7 22.4 %copy-start.5 = (bf16[1,256,1536]{2,1,0:T(8,128)(2,1)S(1)}, bf16[1,256,1536]{2,1,0:T(8,128)(2,1)}, u32[]{:S(2)}) copy-start(bf16[1,256,1536]{2,1,0:T(8,128)(2,1)} %param.23) | copy-start | bytes 2359300
  8.7 232.5 %all-gather.13.cloned.1.call-start = ((), (), s32[]{:S(2)}) async-start(), calls=%async_computation.13 | async-start | bytes 5308416 | tf_op jit(solution)/shard_map/all_gather | solution.py:102
  9.4 245.5 %all-gather.17.cloned.1.call-start = ((), (), s32[]{:S(2)}) async-start(), calls=%async_computation.15 | async-start | bytes 5308416 | tf_op jit(solution)/shard_map/all_gather | solution.py:111
  10.0 343.6 %all-gather.19.cloned.1.call-start = ((), (), s32[]{:S(2)}) async-start(), calls=%async_computation.16 | async-start | bytes 21233664 | tf_op jit(solution)/shard_map/all_gather | solution.py:117
  10.6 443.3 %all-gather.21.cloned.1.call-start = ((), (), s32[]{:S(2)}) async-start(), calls=%async_computation.17 | async-start | bytes 21233664 | tf_op jit(solution)/shard_map/all_gather | solution.py:118
  31.1 69.6 %copy-start.52 = (f32[1536]{0:T(1024)}, f32[1536]{0:T(1024)S(1)}, u32[]{:S(2)}) copy-start(f32[1536]{0:T(1024)S(1)} %get-tuple-element.203) | copy-start | bytes 18436
  31.1 69.6 %copy-start.63 = (f32[1536]{0:T(1024)}, f32[1536]{0:T(1024)S(1)}, u32[]{:S(2)}) copy-start(f32[1536]{0:T(1024)S(1)} %get-tuple-element.163) | copy-start | bytes 18436
  31.1 214.3 %copy-start.65 = (f32[1536]{0:T(1024)}, f32[1536]{0:T(1024)S(1)}, u32[]{:S(2)}) copy-start(f32[1536]{0:T(1024)S(1)} %get-tuple-element.204) | copy-start | bytes 18436
  31.1 214.3 %copy-start.81 = (f32[1536]{0:T(1024)}, f32[1536]{0:T(1024)S(1)}, u32[]{:S(2)}) copy-start(f32[1536]{0:T(1024)S(1)} %get-tuple-element.162) | copy-start | bytes 18436
  31.3 69.4 %copy-start.67 = (f32[256]{0:T(256)}, f32[256]{0:T(256)S(1)}, u32[]{:S(2)}) copy-start(f32[256]{0:T(256)S(1)} %broadcast_multiply_fusion.2) | copy-start | bytes 3076
  31.7 69.0 %copy-start.75 = (f32[256]{0:T(256)}, f32[256]{0:T(256)S(1)}, u32[]{:S(2)}) copy-start(f32[256]{0:T(256)S(1)} %fusion.53) | copy-start | bytes 3076
  31.7 69.0 %copy-start.69 = (f32[256]{0:T(256)}, f32[256]{0:T(256)S(1)}, u32[]{:S(2)}) copy-start(f32[256]{0:T(256)S(1)} %fusion.100) | copy-start | bytes 3076
  104.3 76.6 %all-to-all-start = ((bf16[3,1,256,1536]{2,0,1,3:T(4,128)(2,1)}), bf16[3,1,256,1536]{2,0,1,3:T(4,128)(2,1)}, u32[]{:S(2)}, u32[]{:S(2)}) async-start(bf16[3,1,256,1536]{2,0,1,3:T(4,128)(2,1)} %copy.190), calls=%async_computation | async-start | bytes 6291456 | tf_op jit(solution)/shard_map/all_to_all | solution.py:145
  187.5 8.8 copy-start.27
  189.5 14.1 copy-start.37
  216.4 23.4 %all-to-all-start.1 = ((bf16[4,2,49152]{2,1,0:T(2,128)(2,1)}), bf16[4,2,49152]{2,1,0:T(2,128)(2,1)S(1)}, u32[]{:S(2)}, u32[]{:S(2)}) async-start(bf16[4,2,49152]{2,1,0:T(2,128)(2,1)} %reshape.955), calls=%async_computation.1 | async-start | bytes 1572864 | tf_op jit(solution)/shard_map/all_to_all | solution.py:150
  219.9 320.2 %all-reduce.7.cloned.1.call-start = ((), (), s32[]{:S(2)}) async-start(), calls=%async_computation.18 | async-start | bytes 786432 | tf_op jit(solution)/shard_map/psum | solution.py:212
  252.4 240.4 %copy-start.54 = (f32[24,256]{1,0:T(8,128)}, f32[24,256]{1,0:T(8,128)S(1)}, u32[]{:S(2)}) copy-start(f32[24,256]{1,0:T(8,128)S(1)} %get-tuple-element.188) | copy-start | bytes 73732
  259.5 357.1 %copy-start.8 = (f32[1,256,1536]{2,1,0:T(8,128)}, f32[1,256,1536]{2,1,0:T(8,128)S(1)}, u32[]{:S(2)}) copy-start(f32[1,256,1536]{2,1,0:T(8,128)S(1)} %get-tuple-element.191) | copy-start | bytes 4718596
  259.5 220.4 %copy-start.61 = (f32[256]{0:T(256)}, f32[256]{0:T(256)S(1)}, u32[]{:S(2)}) copy-start(f32[256]{0:T(256)S(1)} %broadcast_multiply_fusion) | copy-start | bytes 3076
  259.9 220.1 %copy-start.71 = (f32[256]{0:T(256)}, f32[256]{0:T(256)S(1)}, u32[]{:S(2)}) copy-start(f32[256]{0:T(256)S(1)} %fusion.102) | copy-start | bytes 3076
  353.6 100.4 %copy-start.21 = (bf16[1,256,1536]{2,1,0:T(8,128)(2,1)S(1)}, bf16[1,256,1536]{2,1,0:T(8,128)(2,1)}, u32[]{:S(2)}) copy-start(bf16[1,256,1536]{2,1,0:T(8,128)(2,1)} %param.33) | copy-start | bytes 2359300
  503.0 404.0 %reduce-scatter.31.cloned.1.call-start = ((), (), s32[]{:S(2)}) async-start(), calls=%async_computation.27 | async-start | bytes 15925248
  598.3 317.9 %reduce-scatter.19.cloned.1.call-start = ((), (), s32[]{:S(2)}) async-start(), calls=%async_computation.20 | async-start | bytes 5308416 | tf_op jit(solution)/shard_map/reduce_scatter | solution.py:224
  603.4 312.9 %reduce-scatter.17.cloned.1.call-start = ((), (), s32[]{:S(2)}) async-start(), calls=%async_computation.19 | async-start | bytes 5308416 | tf_op jit(solution)/shard_map/reduce_scatter | solution.py:252
  616.6 329.1 %reduce-scatter.21.cloned.1.call-start = ((), (), s32[]{:S(2)}) async-start(), calls=%async_computation.21 | async-start | bytes 21233664 | tf_op jit(solution)/shard_map/reduce_scatter | solution.py:189
  629.0 446.6 %reduce-scatter.23.cloned.1.call-start = ((), (), s32[]{:S(2)}) async-start(), calls=%async_computation.22 | async-start | bytes 21233664 | tf_op jit(solution)/shard_map/reduce_scatter | solution.py:192
  648.2 13.8 copy-start.56
  648.2 13.8 copy-start.58
  648.2 13.8 copy-start.51
  648.3 13.8 copy-start.60
  657.4 23.4 %all-to-all-start.2 = ((bf16[4,2,49152]{2,1,0:T(2,128)(2,1)}), bf16[4,2,49152]{2,1,0:T(2,128)(2,1)S(1)}, u32[]{:S(2)}, u32[]{:S(2)}) async-start(bf16[4,2,49152]{2,1,0:T(2,128)(2,1)} %reshape.957), calls=%async_computation.2 | async-start | bytes 1572864 | tf_op jit(solution)/shard_map/all_to_all | solution.py:234
  662.0 519.0 %reduce-scatter.29.cloned.1.call-start = ((), (), s32[]{:S(2)}) async-start(), calls=%async_computation.26 | async-start | bytes 15925248
  683.2 13.3 copy-start.22
  687.5 9.1 copy-start.44
  696.5 14.5 slice-start
  696.5 14.5 slice-start.1
  891.6 326.2 %reduce-scatter.25.cloned.1.call-start = ((), (), s32[]{:S(2)}) async-start(), calls=%async_computation.24 | async-start | bytes 442368
  905.9 348.7 %reduce-scatter.27.cloned.1.call-start = ((), (), s32[]{:S(2)}) async-start(), calls=%async_computation.25 | async-start | bytes 442368
  906.9 586.6 %all-reduce.9.cloned.1.call-start = ((), (), s32[]{:S(2)}) async-start(), calls=%async_computation.28 | async-start | bytes 13369344 | tf_op jit(solution)/shard_map/psum | solution.py:268
  910.8 164.9 %copy-start.19 = (bf16[192,3,1536]{2,1,0:T(4,128)(2,1)}, bf16[192,3,1536]{2,1,0:T(4,128)(2,1)S(1)}, u32[]{:S(2)}) copy-start(bf16[192,3,1536]{2,1,0:T(4,128)(2,1)S(1)} %reshape.948) | copy-start | bytes 5308420
  1075.6 546.4 %all-gather.23.cloned.1.call-start = ((), (), s32[]{:S(2)}) async-start(), calls=%async_computation.23 | async-start | bytes 8847360 | tf_op jit(solution)/shard_map/all_gather | solution.py:264
  1189.6 10.9 copy-start.45
  1208.1 60.6 %copy-start.20 = (bf16[192,3,1536]{2,1,0:T(4,128)(2,1)S(1)}, bf16[192,3,1536]{2,1,0:T(4,128)(2,1)}, u32[]{:S(2)}) copy-start(bf16[192,3,1536]{2,1,0:T(4,128)(2,1)} %copy-done.19) | copy-start | bytes 5308420
  (62 other events, 221.0 us)
Sparse Core Ops, SparseCore 0:
  9.9 81.4 all-gather.10
  93.3 78.6 all-gather.14
  173.8 38.7 all-gather.12
  214.4 38.7 all-gather.16
  254.9 98.5 all-gather.18
  355.3 98.5 all-gather.20
  503.1 36.9 all-reduce.6
  598.4 101.5 reduce-scatter.30
  704.0 53.7 reduce-scatter.18
  761.7 53.7 reduce-scatter.16
  819.2 126.4 reduce-scatter.20
  949.1 126.4 reduce-scatter.22
  1079.2 101.7 reduce-scatter.28
  1183.9 33.8 reduce-scatter.24
  1220.7 33.8 reduce-scatter.26
  1257.8 235.6 all-reduce.8
  1494.9 127.0 all-gather.22
